TPU v7x, 256 devices: a whole 4x4x8 slice. The times are simulated.
256 devices in a mesh: dp: 32 (over z, x_hi, core), tensor: 8 (over y, x_lo).
Axes of the slice: x: 4 (x_hi: 2, x_lo: 2; x = x_hi * 2 + x_lo), y: 4, z: 8, core: 2. Of those that a mesh axis runs over, the one named last changes fastest.
Arguments:
- grads: bfloat16 [32, 40, 128, 4096], P('dp', None, None, 'tensor'), may hold values from -6 to 6
- owner: int32 [40], replicated, may hold values from 0 to 31, as said below
- momentum: float32 [32, 2, 128, 4096], P('dp', None, None, 'tensor'), may hold values from -6 to 6, as said below
Outputs:
- update: bfloat16 [40, 128, 4096], P(None, None, 'tensor')
- new_momentum: float32 [32, 2, 128, 4096], P('dp', None, None, 'tensor')
Inputs may be any that keep to these rules, and one draw needn't show every extreme that they name: Every owner holds at least one matrix and no owner holds more than 2; some owner holds exactly 2. Slot s of owner p holds the momentum of the matrix of slot_rank s among those that owner p holds; slots beyond an owner's count hold values that are carried over.
All inputs are finite; a program needn't handle non-finite values.
Results may differ from a plain program's by a relative error of at most 0.03.
Values may be sent and summed in bfloat16 or wider, within the bound.
A program may use at most 64 MiB of HBM per device.

v0:
```python
import math
import jax
import jax.numpy as jnp
from jax import lax
from jax.sharding import PartitionSpec as P

R = 128
D = 4096
ITERS = 5
COEF_A = 3.4445
COEF_B = -4.775
COEF_C = 2.0315
EPSILON = 1e-07
DECAY = 0.95


def from_everyone(array, axis):
    copies = jnp.broadcast_to(array, (lax.axis_size(axis), *array.shape))
    return lax.all_to_all(copies, axis, split_axis=0, concat_axis=0, tiled=True)


def joined_along(pieces, dim):
    pieces = jnp.moveaxis(pieces, 0, dim)
    shape = pieces.shape
    return pieces.reshape(*shape[:dim], shape[dim] * shape[dim + 1], *shape[dim + 2 :])


def gathered_copies(array, axis, dim):
    pieces = from_everyone(array, axis)
    return joined_along(pieces, dim)


def next_polynomial(gram):
    gram = lax.optimization_barrier(gram)
    square = jnp.einsum("srt,stu->sru", gram, gram, preferred_element_type=jnp.float32)
    return (COEF_B * gram.astype(jnp.float32) + COEF_C * square).astype(jnp.bfloat16)


def apply_polynomial(polynomial, iterate):
    return COEF_A * iterate.astype(jnp.float32) + jnp.einsum(
        "srt,std->srd", polynomial, iterate, preferred_element_type=jnp.float32
    )


def orthogonalize_gathered(rounded, local_cols, factor):
    gathered = gathered_copies(rounded, "tensor", 2)
    squares = jnp.sum(jnp.square(gathered.astype(jnp.float32)), axis=(1, 2))
    iterate = (gathered.astype(jnp.float32) / (jnp.sqrt(squares)[:, None, None] + EPSILON)).astype(
        jnp.bfloat16
    )
    start = lax.axis_index("tensor") * local_cols
    following = None
    for step in range(ITERS):
        gram = jnp.einsum(
            "srd,std->srt", iterate, iterate, preferred_element_type=jnp.float32
        ).astype(jnp.bfloat16)
        polynomial = next_polynomial(gram)
        if step + 1 < ITERS:
            iterate = apply_polynomial(polynomial, iterate).astype(jnp.bfloat16)
        else:
            own_cols = lax.dynamic_slice_in_dim(iterate, start, local_cols, 2)
            following = apply_polynomial(polynomial, own_cols)
    return (factor * following).astype(jnp.bfloat16)


def per_device(grads, owner, momentum):
    owner_count = lax.axis_size("dp")
    myself = lax.axis_index("dp")
    matrices = owner.shape[0]
    slot_count = momentum.shape[1]
    head_rows = grads.shape[2]
    local_cols = grads.shape[3]
    piece_len = head_rows * local_cols // owner_count
    factor = 0.2 * math.sqrt(max(R, D))
    positions = jnp.arange(matrices, dtype=jnp.int32)
    same_owner = owner[:, None] == owner[None, :]
    earlier = positions[None, :] < positions[:, None]
    slot_rank = jnp.sum((same_owner & earlier).astype(jnp.int32), axis=1)
    owner_ids = jnp.arange(owner_count, dtype=jnp.int32)
    slot_ids = jnp.arange(slot_count, dtype=jnp.int32)
    matches = (owner[None, None, :] == owner_ids[:, None, None]) & (
        slot_rank[None, None, :] == slot_ids[None, :, None]
    )
    filled = jnp.any(matches, axis=2)
    source = jnp.sum(jnp.where(matches, positions[None, None, :], 0), axis=2)
    gradient = grads[0]
    zero_float = jnp.zeros((), jnp.float32)
    flattened = gradient.reshape(matrices, head_rows * local_cols).astype(jnp.float32)
    column_part = lax.psum_scatter(
        flattened.astype(jnp.bfloat16), "dp", scatter_dimension=1, tiled=True
    ).astype(jnp.float32)
    outgoing = jnp.take(column_part, source.T.reshape(-1), axis=0).reshape(
        slot_count, owner_count, piece_len
    )
    outgoing = jnp.where(filled.T[:, :, None], outgoing, zero_float)
    incoming = lax.all_to_all(outgoing, "dp", split_axis=1, concat_axis=1, tiled=True)
    mean_grad = incoming.reshape(slot_count, head_rows, local_cols) / owner_count
    previous = momentum[0]
    following = DECAY * previous + mean_grad
    held_here = lax.dynamic_index_in_dim(filled, myself, 0, keepdims=False)
    new_momentum = jnp.where(held_here[:, None, None], following, previous)[None]
    rounded = (mean_grad + DECAY * following).astype(jnp.bfloat16)
    result = orthogonalize_gathered(rounded, local_cols, factor)
    pieces = result.reshape(slot_count, owner_count, piece_len)
    returned = lax.all_to_all(pieces, "dp", split_axis=1, concat_axis=1, tiled=True)
    chosen = jnp.take(
        returned.reshape(slot_count * owner_count, piece_len),
        slot_rank * owner_count + owner,
        axis=0,
    )
    complete = lax.all_gather(chosen, "dp", axis=1, tiled=True)
    update = complete.reshape(matrices, head_rows, local_cols)
    return (update, new_momentum)


def solution(mesh):
    in_specs = (P("dp", None, None, "tensor"), P(), P("dp", None, None, "tensor"))
    out_specs = (P(None, None, "tensor"), P("dp", None, None, "tensor"))
    return jax.shard_map(
        per_device, mesh=mesh, in_specs=in_specs, out_specs=out_specs, check_vma=False
    )
```

profile of v0, /device:TPU:1, one launch (start us, length us, event | category | flops | bytes accessed | tf_op | source)
XLA Modules:
  0.0 357.7 jit_solution(3172155386606064688)
XLA Ops:
  7.2 0.0 reduce-scatter.2.cloned.1.call-start
  7.2 7.9 %copy.34 = bf16[5,8,128,512]{3,1,2,0:T(8,128)(2,1)} copy(bf16[5,8,128,512]{3,2,1,0:T(8,128)(2,1)} %bitcast.51) | data formatting | bytes 10485760
  15.1 0.0 copy-start.4
  15.1 0.0 reduce-scatter.2.cloned.1.call-update
  15.2 0.6 copy-done.4
  15.8 0.2 convert_reduce_fusion
  16.0 0.1 fusion.42
  16.1 0.1 reshape.137
  16.2 0.1 copy.27
  16.3 0.1 and_reduce_fusion
  16.4 0.1 copy.26
  16.5 131.4 %reduce-scatter.2.cloned.1.call-done = bf16[40,2048]{1,0:T(8,128)(2,1)} async-done(((bf16[40,65536]{1,0:T(8,128)(2,1)}), bf16[40,2048]{1,0:T(8,128)(2,1)}) %reduce-scatter.2.cloned.1.call-update) | async-done | bytes 163856 | tf_op jit(solution)/shard_map/reduce_scatter | solution.py:89
  147.9 0.9 convert_element_type.104
  148.9 0.8 gather_fusion
  149.6 0.0 copy-start.3
  149.7 0.6 fusion.20
  150.3 27.4 %all_to_all.15 = f32[2,32,2048]{2,0,1:T(2,128)S(1)} all-to-all(f32[2,32,2048]{2,0,1:T(2,128)S(1)} %fusion.20), channel_id=1, replica_groups=mesh['dp'=32,'tensor'=8] {'dp'}, dimensions={1} | all-to-all | bytes 1048576 | tf_op jit(solution)/shard_map/all_to_all | solution.py:96
  177.7 0.3 copy_multiply_fusion
  178.0 0.1 div.20
  178.2 0.0 copy-done.3
  178.2 0.1 fusion.19
  178.3 1.5 broadcast_in_dim.79
  179.8 4.9 %all-to-all-start.1 = ((bf16[8,2,128,512]{3,2,1,0:T(8,128)(2,1)}), bf16[8,2,128,512]{3,2,1,0:T(8,128)(2,1)S(1)}, u32[]{:S(2)}, u32[]{:S(2)}) async-start(bf16[8,2,128,512]{3,2,1,0:T(8,128)(2,1)} %broadcast_in_dim.79), calls=%async_computation.2 | async-start | bytes 4194304 | tf_op jit(solution)/shard_map/all_to_all | solution.py:19
  184.8 25.7 %all-to-all-done.1 = bf16[8,2,128,512]{3,2,1,0:T(8,128)(2,1)S(1)} async-done(((bf16[8,2,128,512]{3,2,1,0:T(8,128)(2,1)}), bf16[8,2,128,512]{3,2,1,0:T(8,128)(2,1)S(1)}, u32[]{:S(2)}, u32[]{:S(2)}) %all-to-all-start.1) | async-done | bytes 2097184 | tf_op jit(solution)/shard_map/all_to_all | solution.py:19
  210.4 0.7 fusion.4
  211.1 0.6 convert_bitcast_fusion
  211.7 0.6 copy.33
  212.3 0.4 divide_convert_fusion
  212.7 0.7 convolution_convert_fusion.4
  213.4 2.2 fusion
  215.7 0.0 copy-start
  215.7 3.1 convolution_convert_fusion.3
  218.7 0.0 copy-done
  218.8 2.2 fusion.1
  221.0 0.0 copy-start.1
  221.0 3.1 convolution_convert_fusion.2
  224.1 0.0 copy-done.1
  224.1 2.2 fusion.2
  226.3 0.0 copy-start.2
  226.3 3.1 convolution_convert_fusion.1
  229.4 0.0 copy-done.2
  229.4 2.2 fusion.3
  231.6 2.9 convolution_convert_fusion
  234.6 1.4 fusion.6
  236.0 0.2 reshape.138
  236.2 1.0 copy.31
  237.2 7.8 %all-to-all-start.2 = ((bf16[2,32,2048]{2,0,1:T(2,128)(2,1)}), bf16[2,32,2048]{2,0,1:T(2,128)(2,1)S(1)}, u32[]{:S(2)}, u32[]{:S(2)}) async-start(bf16[2,32,2048]{2,0,1:T(2,128)(2,1)} %copy.31), calls=%async_computation.3 | async-start | bytes 524288 | tf_op jit(solution)/shard_map/all_to_all | solution.py:105
  245.0 0.0 all-gather.2.cloned.1.call-start
  245.1 12.9 %all-to-all-done.2 = bf16[2,32,2048]{2,0,1:T(2,128)(2,1)S(1)} async-done(((bf16[2,32,2048]{2,0,1:T(2,128)(2,1)}), bf16[2,32,2048]{2,0,1:T(2,128)(2,1)S(1)}, u32[]{:S(2)}, u32[]{:S(2)}) %all-to-all-start.2) | async-done | bytes 262176 | tf_op jit(solution)/shard_map/all_to_all | solution.py:105
  257.9 0.1 copy.32
  258.0 0.7 gather_fusion.1
  258.7 0.8 broadcast_select_fusion
  259.5 0.0 all-gather.2.cloned.1.call-update
  259.5 0.2 dynamic-slice_reduce_fusion
  259.7 0.1 div.23
  259.8 1.0 add_select_fusion
  260.8 83.2 %all-gather.2.cloned.1.call-done = bf16[40,65536]{1,0:T(8,128)(2,1)} async-done(((bf16[40,2048]{1,0:T(8,128)(2,1)}), bf16[40,65536]{1,0:T(8,128)(2,1)}) %all-gather.2.cloned.1.call-update) | async-done | bytes 5242896 | tf_op jit(solution)/shard_map/all_gather | solution.py:111
  344.0 6.8 %copy.35 = bf16[5,8,128,512]{3,2,1,0:T(8,128)(2,1)} copy(bf16[5,8,128,512]{3,1,2,0:T(8,128)(2,1)} %bitcast.52) | data formatting | bytes 10485760
  (8 shorter events, 0.1 us)
Async XLA Ops:
  7.2 140.8 %reduce-scatter.2.cloned.1.call-start = ((), (), s32[]{:S(2)}) async-start(), calls=%async_computation.4 | async-start | bytes 5406720 | tf_op jit(solution)/shard_map/reduce_scatter | solution.py:89
  15.1 0.7 copy-start.4
  149.6 28.5 %copy-start.3 = (f32[1,2,128,512]{3,2,1,0:T(8,128)S(1)}, f32[1,2,128,512]{3,2,1,0:T(8,128)}, u32[]{:S(2)}) copy-start(f32[1,2,128,512]{3,2,1,0:T(8,128)} %param.5) | copy-start | bytes 1572868
  179.8 30.6 %all-to-all-start.1 = ((bf16[8,2,128,512]{3,2,1,0:T(8,128)(2,1)}), bf16[8,2,128,512]{3,2,1,0:T(8,128)(2,1)S(1)}, u32[]{:S(2)}, u32[]{:S(2)}) async-start(bf16[8,2,128,512]{3,2,1,0:T(8,128)(2,1)} %broadcast_in_dim.79), calls=%async_computation.2 | async-start | bytes 4194304 | tf_op jit(solution)/shard_map/all_to_all | solution.py:19
  215.7 3.1 copy-start
  221.0 3.1 copy-start.1
  226.3 3.1 copy-start.2
  237.2 20.8 %all-to-all-start.2 = ((bf16[2,32,2048]{2,0,1:T(2,128)(2,1)}), bf16[2,32,2048]{2,0,1:T(2,128)(2,1)S(1)}, u32[]{:S(2)}, u32[]{:S(2)}) async-start(bf16[2,32,2048]{2,0,1:T(2,128)(2,1)} %copy.31), calls=%async_computation.3 | async-start | bytes 524288 | tf_op jit(solution)/shard_map/all_to_all | solution.py:105
  245.0 99.0 %all-gather.2.cloned.1.call-start = ((), (), s32[]{:S(2)}) async-start(), calls=%async_computation.5 | async-start | bytes 5406720 | tf_op jit(solution)/shard_map/all_gather | solution.py:111
Sparse Core Ops, SparseCore 0:
  15.3 132.6 reduce-scatter.1
  259.6 84.3 all-gather.1
where the time goes:
time: 358 us
  waiting for transfers between devices  253 us (71%)
  blocking collectives  27.4 us (8%)
  matrix products  23.2 us (6%)
  local copies, waits for them, and re-layouts  21 us (6%)
  between operations  14.2 us (4%)
  starting transfers between devices  12.9 us (4%)
  other arithmetic  5.8 us (2%)
    reduce_scatter x1, waiting for transfers between devices, per_device(): lax.psum_scatter(flattened.astype(jnp.bfloat16), 'dp', scatter_dimension=...  131 us
    all_gather x1, waiting for transfers between devices, per_device(): complete = lax.all_gather(chosen, 'dp', axis=1, tiled=True)  83.2 us
    all_to_all x1, blocking collectives, per_device(): lax.all_to_all(outgoing, 'dp', split_axis=1, concat_axis=1, tiled=True)  27.4 us
    all_to_all x1, waiting for transfers between devices, from_everyone(): return lax.all_to_all(copies, axis, split_axis=0, concat_axis=0, tiled=True)  25.7 us
    unnamed x12, local copies, waits for them, and re-layouts  15.4 us
    dot_general x5, matrix products, orthogonalize_gathered(): jnp.einsum('srd,std->srt', iterate, iterate, preferred_element_type=jnp.f...  12.9 us
    all_to_all x1, waiting for transfers between devices, per_device(): lax.all_to_all(pieces, 'dp', split_axis=1, concat_axis=1, tiled=True)  12.9 us
    dot_general x5, matrix products, apply_polynomial(): jnp.einsum('srt,std->srd', polynomial, iterate, preferred_element_type=jn...  10.4 us
  transfers between devices with their start and end apart: 4, of which 4 were waited for; matrix products, arithmetic and copies ran while one was open for 1% of the time, Pallas kernels for 0%

commit v1 on v0

--- a/solution.py
+++ b/solution.py
@@ -108,7 +108,9 @@
         slot_rank * owner_count + owner,
         axis=0,
     )
-    complete = lax.all_gather(chosen, "dp", axis=1, tiled=True)
+    complete = jnp.concatenate(
+        lax.all_to_all(jnp.stack([chosen] * lax.axis_size("dp")), "dp", 0, 0), axis=1
+    )
     update = complete.reshape(matrices, head_rows, local_cols)
     return (update, new_momentum)
 

time: 358 us -> 409 us (1.14)
  waiting for transfers between devices: 253 us -> 285 us
  local copies, waits for them, and re-layouts: 21 us -> 34 us
  starting transfers between devices: 12.9 us -> 17.7 us
    all_to_all x0 -> x1, waiting for transfers between devices: none -> 115 us  [per_device(): lax.all_to_all(jnp.stack([chosen] * lax.axis_size('dp')), 'dp', 0, 0)]
    all_gather x1 -> x0, waiting for transfers between devices: 83.2 us -> none  [per_device(): complete = lax.all_gather(chosen, 'dp', axis=1, tiled=True)]
    another operation x0 -> x2, local copies, waits for them, and re-layouts: none -> 12.1 us  [the longest x1 9.1 us: per_device(): update = complete.reshape(matrices, head_rows, local_cols)]
    reshape x0 -> x1, local copies, waits for them, and re-layouts: none -> 7.7 us  [per_device(): jnp.concatenate(lax.all_to_all(jnp.stack([chosen] * lax.axis_size('dp')),...]
    unnamed x12 -> x11, local copies, waits for them, and re-layouts: 15.4 us -> 8.56 us
    all_to_all x0 -> x1, starting transfers between devices: none -> 4.88 us  [per_device(): lax.all_to_all(jnp.stack([chosen] * lax.axis_size('dp')), 'dp', 0, 0)]
where the time goes in v1:
time: 409 us; the launch traced here: 407 us
  waiting for transfers between devices  285 us (70%)
  local copies, waits for them, and re-layouts  34 us (8%)
  blocking collectives  27.4 us (7%)
  matrix products  23.1 us (6%)
  starting transfers between devices  17.7 us (4%)
  between operations  14.2 us (3%)
  other arithmetic  5.13 us (1%)
    reduce_scatter x1, waiting for transfers between devices, per_device(): lax.psum_scatter(flattened.astype(jnp.bfloat16), 'dp', scatter_dimension=...  131 us
    all_to_all x1, waiting for transfers between devices, per_device(): lax.all_to_all(jnp.stack([chosen] * lax.axis_size('dp')), 'dp', 0, 0)  115 us
    all_to_all x1, blocking collectives, per_device(): lax.all_to_all(outgoing, 'dp', split_axis=1, concat_axis=1, tiled=True)  27.4 us
    all_to_all x1, waiting for transfers between devices, from_everyone(): return lax.all_to_all(copies, axis, split_axis=0, concat_axis=0, tiled=True)  25.7 us
    all_to_all x1, waiting for transfers between devices, per_device(): lax.all_to_all(pieces, 'dp', split_axis=1, concat_axis=1, tiled=True)  12.9 us
    dot_general x5, matrix products, orthogonalize_gathered(): jnp.einsum('srd,std->srt', iterate, iterate, preferred_element_type=jnp.f...  12.9 us
    dot_general x5, matrix products, apply_polynomial(): jnp.einsum('srt,std->srd', polynomial, iterate, preferred_element_type=jn...  10.3 us
    another operation x1, local copies, waits for them, and re-layouts, per_device(): update = complete.reshape(matrices, head_rows, local_cols)  9.1 us
  transfers between devices with their start and end apart: 4, of which 4 were waited for; matrix products, arithmetic and copies ran while one was open for 1% of the time, Pallas kernels for 0%

profile of v1, /device:TPU:1, one launch (start us, length us, event | category | flops | bytes accessed | tf_op | source)
XLA Modules:
  0.0 406.7 jit_solution(10990777191001387982)
XLA Ops:
  7.2 0.0 reduce-scatter.2.cloned.1.call-start
  7.2 7.9 %copy.37 = bf16[5,8,128,512]{3,1,2,0:T(8,128)(2,1)} copy(bf16[5,8,128,512]{3,2,1,0:T(8,128)(2,1)} %bitcast.50) | data formatting | bytes 10485760
  15.1 0.0 copy-start.4
  15.1 0.0 reduce-scatter.2.cloned.1.call-update
  15.2 0.6 copy-done.4
  15.8 0.2 convert_reduce_fusion
  16.0 0.1 fusion.42
  16.1 0.1 reshape.145
  16.2 0.1 copy.29
  16.3 0.1 and_reduce_fusion
  16.4 0.1 copy.28
  16.5 131.4 %reduce-scatter.2.cloned.1.call-done = bf16[40,2048]{1,0:T(8,128)(2,1)} async-done(((bf16[40,65536]{1,0:T(8,128)(2,1)}), bf16[40,2048]{1,0:T(8,128)(2,1)}) %reduce-scatter.2.cloned.1.call-update) | async-done | bytes 163856 | tf_op jit(solution)/shard_map/reduce_scatter | solution.py:89
  147.9 0.9 convert_element_type.104
  148.9 0.8 gather_fusion
  149.6 0.0 copy-start.3
  149.7 0.6 fusion.20
  150.3 27.4 %all_to_all.20 = f32[2,32,2048]{2,0,1:T(2,128)S(1)} all-to-all(f32[2,32,2048]{2,0,1:T(2,128)S(1)} %fusion.20), channel_id=1, replica_groups=mesh['dp'=32,'tensor'=8] {'dp'}, dimensions={1} | all-to-all | bytes 1048576 | tf_op jit(solution)/shard_map/all_to_all | solution.py:96
  177.7 0.3 copy_multiply_fusion
  178.0 0.1 div.20
  178.2 0.0 copy-done.3
  178.2 0.1 fusion.19
  178.3 1.5 broadcast_in_dim.79
  179.8 4.9 %all-to-all-start.1 = ((bf16[8,2,128,512]{3,2,1,0:T(8,128)(2,1)}), bf16[8,2,128,512]{3,2,1,0:T(8,128)(2,1)S(1)}, u32[]{:S(2)}, u32[]{:S(2)}) async-start(bf16[8,2,128,512]{3,2,1,0:T(8,128)(2,1)} %broadcast_in_dim.79), calls=%async_computation.2 | async-start | bytes 4194304 | tf_op jit(solution)/shard_map/all_to_all | solution.py:19
  184.8 25.7 %all-to-all-done.1 = bf16[8,2,128,512]{3,2,1,0:T(8,128)(2,1)S(1)} async-done(((bf16[8,2,128,512]{3,2,1,0:T(8,128)(2,1)}), bf16[8,2,128,512]{3,2,1,0:T(8,128)(2,1)S(1)}, u32[]{:S(2)}, u32[]{:S(2)}) %all-to-all-start.1) | async-done | bytes 2097184 | tf_op jit(solution)/shard_map/all_to_all | solution.py:19
  210.4 0.7 fusion.4
  211.1 0.6 convert_bitcast_fusion
  211.7 0.6 copy.36
  212.3 0.4 divide_convert_fusion
  212.7 0.7 convolution_convert_fusion.4
  213.4 2.2 fusion
  215.7 0.0 copy-start
  215.7 3.1 convolution_convert_fusion.3
  218.7 0.0 copy-done
  218.8 2.2 fusion.1
  221.0 0.0 copy-start.1
  221.0 3.1 convolution_convert_fusion.2
  224.1 0.0 copy-done.1
  224.1 2.2 fusion.2
  226.3 0.0 copy-start.2
  226.3 3.1 convolution_convert_fusion.1
  229.4 0.0 copy-done.2
  229.4 2.2 fusion.3
  231.6 2.9 convolution_convert_fusion
  234.6 1.4 fusion.6
  235.9 0.2 reshape.146
  236.1 1.0 copy.33
  237.1 7.9 %all-to-all-start.2 = ((bf16[2,32,2048]{2,0,1:T(2,128)(2,1)}), bf16[2,32,2048]{2,0,1:T(2,128)(2,1)S(1)}, u32[]{:S(2)}, u32[]{:S(2)}) async-start(bf16[2,32,2048]{2,0,1:T(2,128)(2,1)} %copy.33), calls=%async_computation.3 | async-start | bytes 524288 | tf_op jit(solution)/shard_map/all_to_all | solution.py:105
  245.0 12.9 %all-to-all-done.2 = bf16[2,32,2048]{2,0,1:T(2,128)(2,1)S(1)} async-done(((bf16[2,32,2048]{2,0,1:T(2,128)(2,1)}), bf16[2,32,2048]{2,0,1:T(2,128)(2,1)S(1)}, u32[]{:S(2)}, u32[]{:S(2)}) %all-to-all-start.2) | async-done | bytes 262176 | tf_op jit(solution)/shard_map/all_to_all | solution.py:105
  257.9 0.1 copy.34
  258.0 0.7 gather_fusion.1
  258.6 0.1 broadcast_select_fusion
  258.7 3.0 stack.2
  261.8 4.9 %all-to-all-start.3 = ((bf16[32,40,2048]{2,1,0:T(8,128)(2,1)}), bf16[32,40,2048]{2,1,0:T(8,128)(2,1)}, u32[]{:S(2)}, u32[]{:S(2)}) async-start(bf16[32,40,2048]{2,1,0:T(8,128)(2,1)} %stack.2), calls=%async_computation.4 | async-start | bytes 10485760 | tf_op jit(solution)/shard_map/all_to_all | solution.py:112
  266.6 0.2 dynamic-slice_reduce_fusion
  266.8 0.1 div.23
  267.0 1.0 add_select_fusion
  267.9 115.1 %all-to-all-done.3 = bf16[32,40,2048]{2,1,0:T(8,128)(2,1)} async-done(((bf16[32,40,2048]{2,1,0:T(8,128)(2,1)}), bf16[32,40,2048]{2,1,0:T(8,128)(2,1)}, u32[]{:S(2)}, u32[]{:S(2)}) %all-to-all-start.3) | async-done | bytes 5242912 | tf_op jit(solution)/shard_map/all_to_all | solution.py:112
  383.1 7.7 %copy.35 = bf16[40,32,2048]{2,1,0:T(8,128)(2,1)} copy(bf16[40,32,2048]{2,0,1:T(8,128)(2,1)} %bitcast.7) | data formatting | bytes 10485760 | tf_op jit(solution)/shard_map/reshape | solution.py:111
  390.8 9.1 %reshape_reshape.3 = bf16[40,128,512]{2,1,0:T(8,128)(2,1)} reshape(bf16[40,32,2048]{2,1,0:T(8,128)(2,1)} %copy.35) | data formatting | bytes 10485760 | tf_op jit(solution)/shard_map/reshape;reshape | solution.py:114
  (8 shorter events, 0.1 us)
Async XLA Ops:
  7.2 140.8 %reduce-scatter.2.cloned.1.call-start = ((), (), s32[]{:S(2)}) async-start(), calls=%async_computation.5 | async-start | bytes 5406720 | tf_op jit(solution)/shard_map/reduce_scatter | solution.py:89
  15.1 0.7 copy-start.4
  149.6 28.5 %copy-start.3 = (f32[1,2,128,512]{3,2,1,0:T(8,128)S(1)}, f32[1,2,128,512]{3,2,1,0:T(8,128)}, u32[]{:S(2)}) copy-start(f32[1,2,128,512]{3,2,1,0:T(8,128)} %param.5) | copy-start | bytes 1572868
  179.8 30.6 %all-to-all-start.1 = ((bf16[8,2,128,512]{3,2,1,0:T(8,128)(2,1)}), bf16[8,2,128,512]{3,2,1,0:T(8,128)(2,1)S(1)}, u32[]{:S(2)}, u32[]{:S(2)}) async-start(bf16[8,2,128,512]{3,2,1,0:T(8,128)(2,1)} %broadcast_in_dim.79), calls=%async_computation.2 | async-start | bytes 4194304 | tf_op jit(solution)/shard_map/all_to_all | solution.py:19
  215.7 3.1 copy-start
  221.0 3.1 copy-start.1
  226.3 3.1 copy-start.2
  237.1 20.8 %all-to-all-start.2 = ((bf16[2,32,2048]{2,0,1:T(2,128)(2,1)}), bf16[2,32,2048]{2,0,1:T(2,128)(2,1)S(1)}, u32[]{:S(2)}, u32[]{:S(2)}) async-start(bf16[2,32,2048]{2,0,1:T(2,128)(2,1)} %copy.33), calls=%async_computation.3 | async-start | bytes 524288 | tf_op jit(solution)/shard_map/all_to_all | solution.py:105
  261.8 121.3 %all-to-all-start.3 = ((bf16[32,40,2048]{2,1,0:T(8,128)(2,1)}), bf16[32,40,2048]{2,1,0:T(8,128)(2,1)}, u32[]{:S(2)}, u32[]{:S(2)}) async-start(bf16[32,40,2048]{2,1,0:T(8,128)(2,1)} %stack.2), calls=%async_computation.4 | async-start | bytes 10485760 | tf_op jit(solution)/shard_map/all_to_all | solution.py:112
Sparse Core Ops, SparseCore 0:
  15.3 132.6 reduce-scatter.1
